TPU v7x, 32 devices: a whole 2x2x4 slice. The times are simulated.
32 devices in a mesh: grp: 2 (over y), inner: 8 (over z, x), outer: 2 (over core).
Axes of the slice: x: 2, y: 2, z: 4, core: 2. Of those that a mesh axis runs over, the one named last changes fastest.
Arguments:
- tokens: bfloat16 [4, 6144, 4096], P(('grp', 'outer'), 'inner'), parts along dimension 0, may hold values from -6 to 6
- w_in: bfloat16 [4096, 1536], P('inner'), may hold values from -0.09375 to 0.09375
- w_dt: bfloat16 [4096, 16], P('inner'), may hold values from -0.09375 to 0.09375
- conv_w: float32 [4, 1536], replicated, may hold values from -0.6 to 0.6
- conv_b: float32 [1536], replicated, may hold values from -0.5 to 0.5
- dt_bias: float32 [16], replicated, may hold values from -2 to 0
- a_log: float32 [16], replicated
- d_skip: float32 [16], replicated, may hold values from 0.5 to 8
- norm_gain: float32 [1024], replicated, may hold values from 0.1 to 1.9
Outputs:
- mixed: bfloat16 [4, 6144, 1024], P(('grp', 'outer'), 'inner'), parts along dimension 0
- entry_states: float32 [4, 8, 16, 64, 256], P(('grp', 'outer'), 'inner'), parts along dimension 0
There are 2 independent parts, one for each index of `grp`. A program takes and returns all parts, laid end to end along the dimension named above; an argument that names none is the same for every part. Nothing has to cross between parts.
All inputs are finite; a program needn't handle non-finite values.
Results may differ from a plain program's by a relative error of at most 0.004.
Values may be sent and summed in bfloat16 or wider, within the bound.
A program may use at most 192 MiB of HBM per device.

v0:
```python
from functools import partial
import jax
import jax.numpy as jnp
from jax import lax
from jax.sharding import PartitionSpec as P

HEADS = 16
P_SIZE = 64
N = 256
CONV = 4
EPSILON = 1e-05


def passed_along(array, axis, by):
    devices = lax.axis_size(axis)
    return lax.ppermute(array, axis, [(i, (i + by) % devices) for i in range(devices)])


def passed_along_2(value, axis, steps):
    count = lax.axis_size(axis)
    leading, last = (max(0, -steps), min(count, count - steps))
    return lax.ppermute(value, axis, [(source, source + steps) for source in range(leading, last)])


def prefix_2(array, axis, combine, identity):
    devices, index = (lax.axis_size(axis), lax.axis_index(axis))
    everything = jax.tree.map(lambda part: lax.all_gather(part, axis), array)
    start = jax.tree.map(
        lambda part, zero: jnp.broadcast_to(jnp.asarray(zero, part.dtype), part.shape),
        array,
        identity,
    )

    def turn(k, before):
        reached = k < index
        new = combine(before, jax.tree.map(lambda part: part[k], everything))
        return jax.tree.map(lambda a, b: jnp.where(reached, a, b), new, before)

    return lax.fori_loop(0, devices, turn, start)


def spread(block, axis, holder):
    block = jnp.where(lax.axis_index(axis) == holder, block, jnp.zeros_like(block))
    return lax.psum(block, axis)


def combine(earlier, later):
    return (earlier[0] * later[0], later[0][:, None, None] * earlier[1] + later[1])


def prepare_span(projected, dt_raw, tail_rows, conv_w, conv_b, dt_bias, a_log):
    length = projected.shape[0]
    padded = jnp.concatenate([tail_rows, projected], axis=0).astype(jnp.float32)
    conv_sum = conv_b[None, :] + conv_w[0][None, :] * padded[0:length]
    for offset in range(1, CONV):
        conv_sum = conv_sum + conv_w[offset][None, :] * padded[offset : offset + length]
    conv_out = jax.nn.silu(conv_sum).astype(jnp.bfloat16)
    inputs = conv_out[:, : HEADS * P_SIZE].reshape(length, HEADS, P_SIZE).transpose(1, 0, 2)
    b_rows = conv_out[:, HEADS * P_SIZE : HEADS * P_SIZE + N]
    c_rows = conv_out[:, HEADS * P_SIZE + N :]
    step_size = jax.nn.softplus(dt_raw.astype(jnp.float32) + dt_bias[None, :]).T
    log_decay = jnp.cumsum(step_size * (-jnp.exp(a_log))[:, None], axis=1)
    return (inputs, b_rows, c_rows, step_size, log_decay)


def span_state(inputs, b_rows, step_size, log_decay):
    final_log = log_decay[:, -1:]
    weighted = (
        (jnp.exp(final_log - log_decay) * step_size)[:, :, None] * inputs.astype(jnp.float32)
    ).astype(jnp.bfloat16)
    contrib = jnp.einsum("hqp,qn->hpn", weighted, b_rows, preferred_element_type=jnp.float32)
    return (jnp.exp(log_decay[:, -1]), contrib)


def head_rows(c_rows, scores, operands):
    log_h, input_h, step_h, entry_h, skip_h, gain_h = operands
    length = log_h.shape[0]
    row_ids = lax.broadcasted_iota(jnp.int32, (length, length), 0)
    col_ids = lax.broadcasted_iota(jnp.int32, (length, length), 1)
    causal = col_ids <= row_ids
    log_gap = jnp.where(causal, log_h[:, None] - log_h[None, :], 0.0)
    mixing = jnp.where(causal, scores * jnp.exp(log_gap), 0.0).astype(jnp.bfloat16)
    driven = (step_h[:, None] * input_h.astype(jnp.float32)).astype(jnp.bfloat16)
    output = jnp.dot(mixing, driven, preferred_element_type=jnp.float32)
    carried = jnp.dot(c_rows, entry_h.astype(jnp.bfloat16).T, preferred_element_type=jnp.float32)
    output = output + jnp.exp(log_h)[:, None] * carried + skip_h * input_h.astype(jnp.float32)
    inv_rms = lax.rsqrt(jnp.mean(output * output, axis=1, keepdims=True) + EPSILON)
    return output * inv_rms * gain_h[None, :]


def span_output(inputs, b_rows, c_rows, step_size, log_decay, entry_state, d_skip, norm_gain):
    scores = jnp.dot(c_rows, b_rows.T, preferred_element_type=jnp.float32)
    head_gains = norm_gain.reshape(HEADS, P_SIZE)
    per_head = lax.map(
        partial(head_rows, c_rows, scores),
        (log_decay, inputs, step_size, entry_state, d_skip, head_gains),
    )
    return per_head.transpose(1, 0, 2).reshape(inputs.shape[1], HEADS * P_SIZE).astype(jnp.bfloat16)


def per_device(tokens, w_in, w_dt, conv_w, conv_b, dt_bias, a_log, d_skip, norm_gain):
    own_rows = tokens.reshape(tokens.shape[1], tokens.shape[2])
    row_count = own_rows.shape[0]
    sums_x = jnp.dot(
        own_rows,
        lax.all_gather(w_in, "inner", axis=0, tiled=True),
        preferred_element_type=jnp.float32,
    )
    sums_dt = jnp.dot(
        own_rows,
        lax.all_gather(w_dt, "inner", axis=0, tiled=True),
        preferred_element_type=jnp.float32,
    )
    projected = sums_x.astype(jnp.bfloat16)
    dt_raw = sums_dt.astype(jnp.bfloat16)
    tail_rows = projected[row_count - CONV + 1 :]
    before = passed_along(tail_rows, "inner", 1)
    prior_block = passed_along_2(before, "outer", 1)
    tail_in = jnp.where(lax.axis_index("inner") == 0, prior_block, before)
    inputs, b_rows, c_rows, step_size, log_decay = prepare_span(
        projected, dt_raw, tail_in, conv_w, conv_b, dt_bias, a_log
    )
    decay_total, contrib = span_state(inputs, b_rows, step_size, log_decay)
    neutral = (jnp.ones_like(decay_total), jnp.zeros_like(contrib))
    prefix = prefix_2((decay_total, contrib), "inner", combine, neutral)
    inclusive = combine(prefix, (decay_total, contrib))
    block_factor, block_state = (
        spread(inclusive[0], "inner", lax.axis_size("inner") - 1),
        spread(inclusive[1], "inner", lax.axis_size("inner") - 1),
    )
    carried = prefix_2((block_factor, block_state), "outer", combine, neutral)
    entry_state = prefix[0][:, None, None] * carried[1] + prefix[1]
    output = span_output(
        inputs, b_rows, c_rows, step_size, log_decay, entry_state, d_skip, norm_gain
    )
    return (
        output.reshape(1, row_count, HEADS * P_SIZE),
        entry_state.reshape(1, 1, HEADS, P_SIZE, N),
    )


def solution(mesh):
    placed = (
        P(("grp", "outer"), "inner", None),
        P("inner", None),
        P("inner", None),
        P(),
        P(),
        P(),
        P(),
        P(),
        P(),
    )
    return jax.shard_map(
        per_device,
        mesh=mesh,
        in_specs=placed,
        out_specs=(
            P(("grp", "outer"), "inner", None),
            P(("grp", "outer"), "inner", None, None, None),
        ),
        check_vma=False,
    )
```

profile of v0, /device:TPU:0, one launch (start us, length us, event | category | flops | bytes accessed | tf_op | source)
XLA Modules:
  0.0 560.5 jit_solution(3436994355984477032)
XLA Ops:
  7.9 33.9 %all_gather.28 = bf16[4096,16]{0,1:T(8,128)(2,1)S(1)} all-gather(bf16[512,16]{0,1:T(8,128)(2,1)} %param.17), channel_id=1, replica_groups=mesh['grp'=2,'inner'=8,'outer'=2] {'inner'}, dimensions={0}, use_global_device_ids=true | all-gather | bytes 147456 | tf_op jit(solution)/shard_map/all_gather | solution.py:111
  42.5 4.6 compare_select_fusion
  47.2 1.7 reduce-window.6
  49.4 140.2 %all-gather.7.cloned.1.call-done = bf16[4096,1536]{1,0:T(8,128)(2,1)} async-done(((bf16[512,1536]{1,0:T(8,128)(2,1)}), bf16[4096,1536]{1,0:T(8,128)(2,1)}) %all-gather.7.cloned.1.call-update) | async-done | bytes 12582928 | tf_op jit(solution)/shard_map/all_gather | solution.py:106
  189.6 14.7 %fusion.25 = bf16[768,1536]{1,0:T(8,128)(2,1)S(1)} fusion(bf16[4096,1536]{1,0:T(8,128)(2,1)} %all-gather.7.cloned.1.call-done, bf16[1,768,4096]{2,1,0:T(8,128)(2,1)} %param.15), kind=kOutput, calls=%fused_computation.46 | convolution fusion | flops 9664856064 | bytes 21233664 | tf_op jit(solution)/shard_map/dot_general | solution.py:104
  205.0 5.7 %collective-permute-done = bf16[3,1536]{1,0:T(4,128)(2,1)S(1)} collective-permute-done((bf16[3,1536]{1,0:T(4,128)(2,1)S(1)}, bf16[3,1536]{1,0:T(4,128)(2,1)S(1)}, u32[]{:S(2)}, u32[]{:S(2)}) %collective-permute-start) | collective-permute-done | bytes 9248 | tf_op jit(solution)/shard_map/ppermute | solution.py:16
  210.8 1.3 collective-permute-start.1
  213.6 3.0 multiply_convert_fusion
  216.7 1.6 slice.69
  218.2 2.6 copy.21
  220.8 3.0 fusion.28
  225.3 17.8 %all-reduce = f32[128]{0:T(128)S(1)} all-reduce(f32[128]{0:T(128)S(1)} %dynamic-update-slice), channel_id=2, replica_groups=mesh['grp'=2,'inner'=8,'outer'=2] {'inner'}, use_global_device_ids=true, to_apply=%add | all-reduce | flops 128 | bytes 1024
  243.2 102.7 %all-gather.11.cloned.1.call-done = f32[128,64,256]{2,1,0:T(8,128)} async-done(((f32[16,64,256]{2,1,0:T(8,128)}), f32[128,64,256]{2,1,0:T(8,128)}) %all-gather.11.cloned.1.call-update) | async-done | bytes 8388624 | tf_op jit(solution)/shard_map/all_gather | solution.py:27
  345.8 12.1 %while.41 = (s32[]{:T(128)}, f32[16]{0:T(128)S(1)}, f32[16,64,256]{2,1,0:T(8,128)S(1)}, s32[]{:T(128)}, f32[8,16]{1,0:T(8,128)S(1)}, /*index=5*/f32[8,16,64,256]{3,2,1,0:T(8,128)}, s32[]{:T(128)}, s32[]{:T(128)}) while((s32[]{:T(128)}, f32[16]{0:T(128)S(1)}, f32[16,64,256]{2,1,0:T(8,128)S(1)}, s32[]{:T(128)}, ...), condition=%wide.region_3.4_spmd.clone, body=%wide.region_2.3_spmd.clone.sunk | while | flops 1048628 | bytes 3146163 | solution.py:39
  345.9 1.5 fusion.62
  347.4 1.5 fusion.62
  349.0 1.5 fusion.62
  350.5 1.5 fusion.62
  352.0 1.5 fusion.62
  353.5 1.5 fusion.62
  355.0 1.5 fusion.62
  356.5 1.5 fusion.62
  359.2 76.5 %all-reduce.3.cloned.1.call-done = f32[1,16,64,256]{3,2,1,0:T(8,128)} async-done(((f32[1,16,64,256]{3,2,1,0:T(8,128)}), f32[1,16,64,256]{3,2,1,0:T(8,128)}) %all-reduce.3.cloned.1.call-update) | async-done | bytes 1048592 | tf_op jit(solution)/shard_map/psum | solution.py:44
  435.9 3.0 fusion.41
  438.9 20.0 %psum.14 = f32[1,16]{1,0:T(1,128)S(1)} all-reduce(f32[1,16]{1,0:T(1,128)S(1)} %get-tuple-element.362), channel_id=1, replica_groups=mesh['grp'=2,'inner'=8,'outer'=2] {'inner'}, use_global_device_ids=true, to_apply=%region_4.5 | all-reduce | flops 16 | bytes 128 | tf_op jit(solution)/shard_map/psum | solution.py:44
  458.9 1.8 all-gather.2
  460.7 3.0 while.42
  460.8 1.5 fusion.63
  462.3 1.5 fusion.63
  463.8 1.2 fusion.47
  464.9 86.4 %while.40 = (s32[]{:T(128)}, bf16[16,768,64]{1,2,0:T(8,128)(2,1)}, f32[16,768]{1,0:T(8,128)S(1)}, f32[768,768]{1,0:T(8,128)}, f32[16,768]{1,0:T(8,128)S(1)}, /*i...) while((s32[]{:T(128)}, bf16[16,768,64]{1,2,0:T(8,128)(2,1)}, ...), condition=%wide.region_10.11_spmd, body=%wide.region_8.10_spmd.sunk | while | flops 104792832 | bytes 4015489 | solution.py:94
  464.9 2.2 fusion.60
  467.7 1.8 multiply_reduce_fusion.2
  470.3 2.2 fusion.60
  473.1 1.8 multiply_reduce_fusion.2
  475.7 2.2 fusion.60
  478.5 1.8 multiply_reduce_fusion.2
  481.2 2.2 fusion.60
  483.9 1.8 multiply_reduce_fusion.2
  486.6 2.2 fusion.60
  489.4 1.8 multiply_reduce_fusion.2
  492.0 2.2 fusion.60
  494.8 1.8 multiply_reduce_fusion.2
  497.4 2.2 fusion.60
  500.1 1.8 multiply_reduce_fusion.2
  502.8 2.2 fusion.60
  505.5 1.8 multiply_reduce_fusion.2
  508.2 2.2 fusion.60
  511.0 1.8 multiply_reduce_fusion.2
  513.6 2.2 fusion.60
  516.4 1.8 multiply_reduce_fusion.2
  519.0 2.2 fusion.60
  521.8 1.8 multiply_reduce_fusion.2
  524.4 2.2 fusion.60
  527.2 1.8 multiply_reduce_fusion.2
  529.8 2.2 fusion.60
  532.6 1.8 multiply_reduce_fusion.2
  535.2 2.2 fusion.60
  538.0 1.8 multiply_reduce_fusion.2
  540.6 2.2 fusion.60
  543.4 1.8 multiply_reduce_fusion.2
  546.0 2.2 fusion.60
  548.8 1.8 multiply_reduce_fusion.2
  551.4 2.6 copy.22
  (155 shorter events, 28.3 us)
Async XLA Ops:
  7.2 182.4 %all-gather.7.cloned.1.call-start = ((), (), s32[]{:S(2)}) async-start(), calls=%async_computation | async-start | bytes 14155776 | tf_op jit(solution)/shard_map/all_gather | solution.py:106
  7.9 337.9 %all-gather.11.cloned.1.call-start = ((), (), s32[]{:S(2)}) async-start(), calls=%async_computation.3 | async-start | bytes 9437184 | tf_op jit(solution)/shard_map/all_gather | solution.py:27
  49.4 162.7 %copy-start.2 = (f32[4,1536]{1,0:T(4,128)S(1)}, f32[4,1536]{1,0:T(4,128)}, u32[]{:S(2)}) copy-start(f32[4,1536]{1,0:T(4,128)} %param.18) | copy-start | bytes 73732
  204.3 6.4 %collective-permute-start = (bf16[3,1536]{1,0:T(4,128)(2,1)S(1)}, bf16[3,1536]{1,0:T(4,128)(2,1)S(1)}, u32[]{:S(2)}, u32[]{:S(2)}) collective-permute-start(bf16[3,1536]{1,0:T(4,128)(2,1)S(1)} %slice.62), channel_id=1, source_target_pairs={{0,2},{2,4},{4,6},{6,8},{8,10},{10,12},{12,14},{14,0},{1,3},{3,5},... | collective-permute-start | bytes 27656 | tf_op jit(solution)/shard_map/ppermute | solution.py:16
  210.8 2.1 collective-permute-start.1
  212.9 0.7 copy-start.3
  216.7 4.2 copy-start
  220.8 3.1 copy-start.6
  223.8 211.9 %all-reduce.3.cloned.1.call-start = ((), (), s32[]{:S(2)}) async-start(), calls=%async_computation.1 | async-start | bytes 2097152 | tf_op jit(solution)/shard_map/psum | solution.py:44
  345.8 12.1 %copy-start.1 = (f32[16,64,256]{2,1,0:T(8,128)S(1)}, f32[16,64,256]{2,1,0:T(8,128)}, u32[]{:S(2)}) copy-start(f32[16,64,256]{2,1,0:T(8,128)} %fusion.28) | copy-start | bytes 3145732
  358.0 77.8 %copy-start.4 = (f32[1024]{0:T(1024)S(1)}, f32[1024]{0:T(1024)}, u32[]{:S(2)}) copy-start(f32[1024]{0:T(1024)} %param.23) | copy-start | bytes 12292
  359.2 101.6 %all-gather.9.cloned.1.call-start = ((), (), s32[]{:S(2)}) async-start(), calls=%async_computation.2 | async-start | bytes 3145728 | tf_op jit(solution)/shard_map/all_gather | solution.py:27
  463.7 1.2 slice-start
  463.7 1.2 copy-start.5
Sparse Core Ops, SparseCore 0:
  10.2 179.3 all-gather.6
  223.9 121.8 all-gather.10
  359.3 76.4 all-reduce.2
  437.2 10.1 all-gather.8
where the time goes:
time: 562 us; the launch traced here: 560 us
  waiting for transfers between devices  327 us (58%)
  matrix products  89.3 us (16%)
  blocking collectives  73.6 us (13%)
  other arithmetic  35.2 us (6%)
  local copies, waits for them, and re-layouts  18.3 us (3%)
  between operations  14.6 us (3%)
    all_gather x1, waiting for transfers between devices, per_device(): lax.all_gather(w_in, 'inner', axis=0, tiled=True)  140 us
    all_gather x2, waiting for transfers between devices, prefix_2(): everything = jax.tree.map(lambda part: lax.all_gather(part, axis), array)  103 us
    psum x1, waiting for transfers between devices, spread(): return lax.psum(block, axis)  76.5 us
    dot_general x16, matrix products, head_rows(): output = jnp.dot(mixing, driven, preferred_element_type=jnp.float32)  35 us
    all_gather x1, blocking collectives, per_device(): lax.all_gather(w_dt, 'inner', axis=0, tiled=True)  33.9 us
    dot_general x16, matrix products, head_rows(): jnp.dot(c_rows, entry_h.astype(jnp.bfloat16).T, preferred_element_type=jn...  29.1 us
    psum x1, blocking collectives, spread(): return lax.psum(block, axis)  20 us
    unnamed x1, blocking collectives  17.8 us
  transfers between devices with their start and end apart: 6, of which 5 were waited for; matrix products, arithmetic and copies ran while one was open for 2% of the time, Pallas kernels for 0%

commit v1 on v0

--- a/solution.py
+++ b/solution.py
@@ -41,7 +41,7 @@
 
 def spread(block, axis, holder):
     block = jnp.where(lax.axis_index(axis) == holder, block, jnp.zeros_like(block))
-    return lax.psum(block, axis)
+    return jnp.sum(lax.all_gather(block, axis), axis=0)
 
 
 def combine(earlier, later):

time: 562 us -> 615 us (1.094)
  waiting for transfers between devices: 327 us -> 373 us
    all_gather x0 -> x1, waiting for transfers between devices: none -> 123 us  [spread(): return jnp.sum(lax.all_gather(block, axis), axis=0)]
    psum x1 -> x0, waiting for transfers between devices: 76.5 us -> none  [spread(): return lax.psum(block, axis)]
    unnamed x1 -> x3, blocking collectives: 17.8 us -> 38.7 us
    psum x1 -> x0, blocking collectives: 20 us -> none  [spread(): return lax.psum(block, axis)]
where the time goes in v1:
time: 615 us; the launch traced here: 613 us
  waiting for transfers between devices  373 us (61%)
  matrix products  89.3 us (15%)
  blocking collectives  72.7 us (12%)
  other arithmetic  40.4 us (7%)
  local copies, waits for them, and re-layouts  19.3 us (3%)
  between operations  15.3 us (2%)
    all_gather x1, waiting for transfers between devices, per_device(): lax.all_gather(w_in, 'inner', axis=0, tiled=True)  140 us
    all_gather x1, waiting for transfers between devices, spread(): return jnp.sum(lax.all_gather(block, axis), axis=0)  123 us
    all_gather x2, waiting for transfers between devices, prefix_2(): everything = jax.tree.map(lambda part: lax.all_gather(part, axis), array)  103 us
    unnamed x3, blocking collectives  38.7 us
    dot_general x16, matrix products, head_rows(): output = jnp.dot(mixing, driven, preferred_element_type=jnp.float32)  35 us
    all_gather x1, blocking collectives, per_device(): lax.all_gather(w_dt, 'inner', axis=0, tiled=True)  33.9 us
    dot_general x16, matrix products, head_rows(): jnp.dot(c_rows, entry_h.astype(jnp.bfloat16).T, preferred_element_type=jn...  29.1 us
    select_n x18, other arithmetic, turn(): return jax.tree.map(lambda a, b: jnp.where(reached, a, b), new, before)  14.8 us
  transfers between devices with their start and end apart: 6, of which 5 were waited for; matrix products, arithmetic and copies ran while one was open for 2% of the time, Pallas kernels for 0%

profile of v1, /device:TPU:0, one launch (start us, length us, event | category | flops | bytes accessed | tf_op | source)
XLA Modules:
  0.0 612.7 jit_solution(5669940397621444973)
XLA Ops:
  7.9 33.9 %all_gather.40 = bf16[4096,16]{0,1:T(8,128)(2,1)S(1)} all-gather(bf16[512,16]{0,1:T(8,128)(2,1)} %param.17), channel_id=1, replica_groups=mesh['grp'=2,'inner'=8,'outer'=2] {'inner'}, dimensions={0}, use_global_device_ids=true | all-gather | bytes 147456 | tf_op jit(solution)/shard_map/all_gather | solution.py:111
  42.5 4.6 compare_select_fusion
  47.2 1.7 reduce-window.6
  49.4 140.2 %all-gather.11.cloned.1.call-done = bf16[4096,1536]{1,0:T(8,128)(2,1)} async-done(((bf16[512,1536]{1,0:T(8,128)(2,1)}), bf16[4096,1536]{1,0:T(8,128)(2,1)}) %all-gather.11.cloned.1.call-update) | async-done | bytes 12582928 | tf_op jit(solution)/shard_map/all_gather | solution.py:106
  189.6 14.7 %fusion.25 = bf16[768,1536]{1,0:T(8,128)(2,1)S(1)} fusion(bf16[4096,1536]{1,0:T(8,128)(2,1)} %all-gather.11.cloned.1.call-done, bf16[1,768,4096]{2,1,0:T(8,128)(2,1)} %param.15), kind=kOutput, calls=%fused_computation.46 | convolution fusion | flops 9664856064 | bytes 21233664 | tf_op jit(solution)/shard_map/dot_general | solution.py:104
  205.0 5.7 collective-permute-done
  210.8 1.3 collective-permute-start.1
  213.6 3.0 multiply_convert_fusion
  216.7 1.6 slice.69
  218.2 2.6 copy.21
  220.8 3.0 fusion.28
  225.4 17.8 %all-reduce = f32[128]{0:T(128)S(1)} all-reduce(f32[128]{0:T(128)S(1)} %dynamic-update-slice), channel_id=2, replica_groups=mesh['grp'=2,'inner'=8,'outer'=2] {'inner'}, use_global_device_ids=true, to_apply=%add | all-reduce | flops 128 | bytes 1024
  243.2 102.6 %all-gather.13.cloned.1.call-done = f32[128,64,256]{2,1,0:T(8,128)} async-done(((f32[16,64,256]{2,1,0:T(8,128)}), f32[128,64,256]{2,1,0:T(8,128)}) %all-gather.13.cloned.1.call-update) | async-done | bytes 8388624 | tf_op jit(solution)/shard_map/all_gather | solution.py:27
  345.8 12.1 %while.41 = (s32[]{:T(128)}, f32[16]{0:T(128)S(1)}, f32[16,64,256]{2,1,0:T(8,128)S(1)}, s32[]{:T(128)}, f32[8,16]{1,0:T(8,128)S(1)}, /*index=5*/f32[8,16,64,256]{3,2,1,0:T(8,128)}, s32[]{:T(128)}, s32[]{:T(128)}) while((s32[]{:T(128)}, f32[16]{0:T(128)S(1)}, f32[16,64,256]{2,1,0:T(8,128)S(1)}, s32[]{:T(128)}, ...), condition=%wide.region_3.4_spmd.clone, body=%wide.region_2.3_spmd.clone.sunk | while | flops 1048628 | bytes 3146163 | solution.py:39
  345.9 1.5 fusion.62
  347.4 1.5 fusion.62
  349.0 1.5 fusion.62
  350.5 1.5 fusion.62
  352.0 1.5 fusion.62
  353.5 1.5 fusion.62
  355.0 1.5 fusion.62
  356.5 1.5 fusion.62
  359.3 122.8 %all-gather.15.cloned.1.call-done = f32[128,64,256]{2,1,0:T(8,128)} async-done(((f32[16,64,256]{2,1,0:T(8,128)}), f32[128,64,256]{2,1,0:T(8,128)}) %all-gather.15.cloned.1.call-update) | async-done | bytes 8388624 | tf_op jit(solution)/shard_map/all_gather | solution.py:44
  482.1 5.1 reduce_sum.28
  488.6 3.0 fusion.41
  491.6 18.5 %all-reduce.1 = f32[128]{0:T(128)S(1)} all-reduce(f32[128]{0:T(128)S(1)} %get-tuple-element.362), channel_id=4, replica_groups=mesh['grp'=2,'inner'=8,'outer'=2] {'inner'}, use_global_device_ids=true, to_apply=%add.1 | all-reduce | flops 128 | bytes 1024
  510.5 2.4 all-reduce.2
  513.0 3.0 while.42
  513.0 1.5 fusion.63
  514.5 1.5 fusion.63
  517.2 86.4 %while.40 = (s32[]{:T(128)}, bf16[16,768,64]{1,2,0:T(8,128)(2,1)}, f32[16,768]{1,0:T(8,128)S(1)}, f32[768,768]{1,0:T(8,128)}, f32[16,768]{1,0:T(8,128)S(1)}, /*i...) while((s32[]{:T(128)}, bf16[16,768,64]{1,2,0:T(8,128)(2,1)}, ...), condition=%wide.region_10.11_spmd, body=%wide.region_8.10_spmd.sunk | while | flops 104792832 | bytes 4015489 | solution.py:94
  517.2 2.2 fusion.60
  520.0 1.8 multiply_reduce_fusion.2
  522.6 2.2 fusion.60
  525.4 1.8 multiply_reduce_fusion.2
  528.0 2.2 fusion.60
  530.8 1.8 multiply_reduce_fusion.2
  533.4 2.2 fusion.60
  536.2 1.8 multiply_reduce_fusion.2
  538.8 2.2 fusion.60
  541.6 1.8 multiply_reduce_fusion.2
  544.2 2.2 fusion.60
  547.0 1.8 multiply_reduce_fusion.2
  549.6 2.2 fusion.60
  552.4 1.8 multiply_reduce_fusion.2
  555.0 2.2 fusion.60
  557.8 1.8 multiply_reduce_fusion.2
  560.4 2.2 fusion.60
  563.2 1.8 multiply_reduce_fusion.2
  565.8 2.2 fusion.60
  568.6 1.8 multiply_reduce_fusion.2
  571.2 2.2 fusion.60
  574.0 1.8 multiply_reduce_fusion.2
  576.6 2.2 fusion.60
  579.4 1.8 multiply_reduce_fusion.2
  582.0 2.2 fusion.60
  584.8 1.8 multiply_reduce_fusion.2
  587.4 2.2 fusion.60
  590.2 1.8 multiply_reduce_fusion.2
  592.8 2.2 fusion.60
  595.6 1.8 multiply_reduce_fusion.2
  598.2 2.2 fusion.60
  601.0 1.8 multiply_reduce_fusion.2
  603.6 2.6 copy.22
  (165 shorter events, 30.7 us)
Async XLA Ops:
  7.2 182.4 %all-gather.11.cloned.1.call-start = ((), (), s32[]{:S(2)}) async-start(), calls=%async_computation | async-start | bytes 14155776 | tf_op jit(solution)/shard_map/all_gather | solution.py:106
  7.9 337.9 %all-gather.13.cloned.1.call-start = ((), (), s32[]{:S(2)}) async-start(), calls=%async_computation.1 | async-start | bytes 9437184 | tf_op jit(solution)/shard_map/all_gather | solution.py:27
  49.4 162.7 %copy-start.2 = (f32[4,1536]{1,0:T(4,128)S(1)}, f32[4,1536]{1,0:T(4,128)}, u32[]{:S(2)}) copy-start(f32[4,1536]{1,0:T(4,128)} %param.18) | copy-start | bytes 73732
  204.3 6.4 %collective-permute-start = (bf16[3,1536]{1,0:T(4,128)(2,1)S(1)}, bf16[3,1536]{1,0:T(4,128)(2,1)S(1)}, u32[]{:S(2)}, u32[]{:S(2)}) collective-permute-start(bf16[3,1536]{1,0:T(4,128)(2,1)S(1)} %slice.62), channel_id=1, source_target_pairs={{0,2},{2,4},{4,6},{6,8},{8,10},{10,12},{12,14},{14,0},{1,3},{3,5},... | collective-permute-start | bytes 27656 | tf_op jit(solution)/shard_map/ppermute | solution.py:16
  210.8 2.1 collective-permute-start.1
  212.9 0.7 copy-start.3
  216.7 4.2 copy-start
  220.8 3.1 copy-start.7
  223.8 258.3 %all-gather.15.cloned.1.call-start = ((), (), s32[]{:S(2)}) async-start(), calls=%async_computation.2 | async-start | bytes 9437184 | tf_op jit(solution)/shard_map/all_gather | solution.py:44
  345.8 12.2 %copy-start.1 = (f32[16,64,256]{2,1,0:T(8,128)S(1)}, f32[16,64,256]{2,1,0:T(8,128)}, u32[]{:S(2)}) copy-start(f32[16,64,256]{2,1,0:T(8,128)} %fusion.28) | copy-start | bytes 3145732
  359.3 153.7 %all-gather.17.cloned.1.call-start = ((), (), s32[]{:S(2)}) async-start(), calls=%async_computation.3 | async-start | bytes 3145728 | tf_op jit(solution)/shard_map/all_gather | solution.py:27
  482.1 5.2 copy-start.6
  482.1 6.5 %copy-start.4 = (f32[1024]{0:T(1024)S(1)}, f32[1024]{0:T(1024)}, u32[]{:S(2)}) copy-start(f32[1024]{0:T(1024)} %param.23) | copy-start | bytes 12292
  516.0 1.2 slice-start
  516.0 1.2 copy-start.5
Sparse Core Ops, SparseCore 0:
  10.2 179.3 all-gather.10
  223.9 121.8 all-gather.12
  359.4 122.6 all-gather.14
  487.4 8.7 all-gather.16
